TPU v7x, 32 devices: a whole 2x2x4 slice. The times are simulated.
32 devices in a mesh: hyd: 4 (over y, x), src: 8 (over z, core).
Axes of the slice: x: 2, y: 2, z: 4, core: 2. Of those that a mesh axis runs over, the one named last changes fastest.
Arguments:
- record: float32 [2, 4096, 128], P(None, 'hyd'), may hold values from -6 to 6
- tile_data: bfloat16 [4, 8, 24, 2, 128, 128], P('hyd', 'src'), may hold values from -0.125 to 0.125
- tile_rows: int32 [4, 8, 24], P('hyd', 'src'), may hold values from 0 to 7, as said below
- tile_cols: int32 [4, 8, 24], P('hyd', 'src'), may hold values from 0 to 7, as said below
- tile_counts: int32 [4, 8], P('hyd', 'src'), may hold values from 3 to 24, as said below
Outputs:
- solution: float32 [2, 8192, 128], P(None, 'src')
- residual: float32 [2, 4096, 128], P(None, 'hyd')
Inputs may be any that keep to these rules, and one draw needn't show every extreme that they name: `tile_rows`: together with tile_cols, the 24 slots of one device name different tile pairs. `tile_cols`: column tiles below 4 belong to the upper layer. `tile_counts`: slots at and beyond a device's count hold no tiles of A.
All inputs are finite; a program needn't handle non-finite values.
Results may differ from a plain program's by a relative error of at most 0.014.
Values may be sent and summed in bfloat16 or wider, within the bound.
No kernel may reach another device: no remote copies, remote signals or barrier semaphores. Data moves between devices by JAX's collectives and lax.ppermute only.
A program may use at most 64 MiB of HBM per device.

v0:
```python
import jax
import jax.numpy as jnp
from jax import lax
from jax.sharding import PartitionSpec as P

SRC_DEV = 512
ITERS = 3
EPSILON = 1e-06


def place_tiles(total, products, target, usable):
    for slot in range(products.shape[1]):
        current = lax.dynamic_slice_in_dim(total, target[slot], 1, 1)
        added = current + products[:, slot][:, None] * usable[slot]
        total = lax.dynamic_update_slice_in_dim(total, added, target[slot], 1)
    return total


def tile_forward(tile_group_all, rows_list, cols_list, first_slot, end_slot, vector_b, row_tiles):
    group_slots = 8
    tile_size = tile_group_all.shape[-1]
    shot_count = vector_b.shape[2]
    col_tiles = vector_b.shape[1] // tile_size
    blocks = vector_b.reshape(2, col_tiles, tile_size, shot_count)

    def one_turn(group, total):
        start = group * group_slots
        tile_group = lax.dynamic_slice_in_dim(tile_group_all, start, group_slots, 0)
        col_pick = lax.dynamic_slice_in_dim(cols_list, start, group_slots, 0)
        row_pick = lax.dynamic_slice_in_dim(rows_list, start, group_slots, 0)
        slot_ids = start + jnp.arange(group_slots)
        usable = ((slot_ids >= first_slot) & (slot_ids < end_slot)).astype(jnp.float32)
        chosen = jnp.take(blocks, col_pick, axis=1)
        real_part = jnp.einsum(
            "gij,gjn->gin", tile_group[:, 0], chosen[0], preferred_element_type=jnp.float32
        ) - jnp.einsum(
            "gij,gjn->gin", tile_group[:, 1], chosen[1], preferred_element_type=jnp.float32
        )
        imag_part = jnp.einsum(
            "gij,gjn->gin", tile_group[:, 0], chosen[1], preferred_element_type=jnp.float32
        ) + jnp.einsum(
            "gij,gjn->gin", tile_group[:, 1], chosen[0], preferred_element_type=jnp.float32
        )
        return place_tiles(total, jnp.stack([real_part, imag_part]), row_pick, usable)

    empty = jnp.zeros((2, row_tiles, tile_size, shot_count), jnp.float32)
    result = lax.fori_loop(
        first_slot // group_slots, (end_slot + group_slots - 1) // group_slots, one_turn, empty
    )
    return result.reshape(2, row_tiles * tile_size, shot_count)


def tile_adjoint(tile_group_all, rows_list, cols_list, first_slot, end_slot, residual_b, col_tiles):
    group_slots = 8
    tile_size = tile_group_all.shape[-1]
    shot_count = residual_b.shape[2]
    row_tiles = residual_b.shape[1] // tile_size
    blocks = residual_b.reshape(2, row_tiles, tile_size, shot_count)

    def one_turn(group, total):
        start = group * group_slots
        tile_group = lax.dynamic_slice_in_dim(tile_group_all, start, group_slots, 0)
        col_pick = lax.dynamic_slice_in_dim(cols_list, start, group_slots, 0)
        row_pick = lax.dynamic_slice_in_dim(rows_list, start, group_slots, 0)
        slot_ids = start + jnp.arange(group_slots)
        usable = ((slot_ids >= first_slot) & (slot_ids < end_slot)).astype(jnp.float32)
        chosen = jnp.take(blocks, row_pick, axis=1)
        real_part = jnp.einsum(
            "gji,gjn->gin", tile_group[:, 0], chosen[0], preferred_element_type=jnp.float32
        ) + jnp.einsum(
            "gji,gjn->gin", tile_group[:, 1], chosen[1], preferred_element_type=jnp.float32
        )
        imag_part = jnp.einsum(
            "gji,gjn->gin", tile_group[:, 0], chosen[1], preferred_element_type=jnp.float32
        ) - jnp.einsum(
            "gji,gjn->gin", tile_group[:, 1], chosen[0], preferred_element_type=jnp.float32
        )
        return place_tiles(total, jnp.stack([real_part, imag_part]), col_pick, usable)

    empty = jnp.zeros((2, col_tiles, tile_size, shot_count), jnp.float32)
    result = lax.fori_loop(
        first_slot // group_slots, (end_slot + group_slots - 1) // group_slots, one_turn, empty
    )
    return result.reshape(2, col_tiles * tile_size, shot_count)


def body(record, tile_data, tile_rows, tile_cols, tile_counts):
    own_tiles = tile_data[0, 0]
    own_rows = tile_rows[0, 0]
    own_cols = tile_cols[0, 0]
    own_count = tile_counts[0, 0]
    tile_size = own_tiles.shape[-1]
    row_tiles = record.shape[1] // tile_size
    col_tiles = 2 * SRC_DEV // tile_size

    def gradient_of(residual_b):
        partial_value = tile_adjoint(
            own_tiles, own_rows, own_cols, 0, own_count, residual_b, col_tiles
        )
        gradient = lax.psum(partial_value, "hyd")
        squares = lax.psum(jnp.sum(gradient * gradient, axis=(0, 1)), "src")
        return (gradient, squares)

    residual = record
    gradient, gamma_now = gradient_of(record.astype(jnp.bfloat16))
    direction = gradient
    solution = jnp.zeros_like(gradient)
    for step_index in range(ITERS):
        direction_b = direction.astype(jnp.bfloat16)
        forward_partial_value = tile_forward(
            own_tiles, own_rows, own_cols, 0, own_count, direction_b, row_tiles
        )
        image = lax.psum(forward_partial_value, "src")
        image_sq = lax.psum(jnp.sum(image * image, axis=(0, 1)), "hyd")
        image, image_sq = (image, image_sq)
        alpha_step = gamma_now / (image_sq + EPSILON)
        solution = solution + alpha_step * direction
        residual = residual - alpha_step * image
        if step_index + 1 < ITERS:
            residual_b = residual.astype(jnp.bfloat16)
            gradient, gamma_next = gradient_of(residual_b)
            direction = gradient + gamma_next / (gamma_now + EPSILON) * direction
            gamma_now = gamma_next
    return (solution, residual)


def solution(mesh):
    in_specs = (
        P(None, "hyd", None),
        P("hyd", "src", None, None, None, None),
        P("hyd", "src", None),
        P("hyd", "src", None),
        P("hyd", "src"),
    )
    out_specs = (P(None, "src", None), P(None, "hyd", None))
    return jax.shard_map(body, mesh=mesh, in_specs=in_specs, out_specs=out_specs, check_vma=False)
```

profile of v0, /device:TPU:0, one launch (start us, length us, event | category | flops | bytes accessed | tf_op | source)
XLA Modules:
  0.0 1104.4 jit_solution(888676539581461893)
XLA Ops:
  7.9 2.7 copy.18
  11.3 28.1 %while.60 = (s32[]{:T(128)}, f32[2,8,128,128]{3,2,1,0:T(8,128)S(1)}, s32[]{:T(128)}, s32[24]{0:T(128)S(1)}, bf16[24,2,128,128]{2,3,0,1:T(8,128)(2,1)}, /*index=5...) while((s32[]{:T(128)}, ...), condition=%wide.region_1.3_spmd, body=%wide.region_0.2_spmd.sunk | while | flops 135529568 | bytes 17830816 | solution.py:81
  41.9 108.4 %all-reduce.7.cloned.1.call-done = f32[2,1024,128]{2,1,0:T(8,128)} async-done(((f32[2,1024,128]{2,1,0:T(8,128)}), f32[2,1024,128]{2,1,0:T(8,128)}) %all-reduce.7.cloned.1.call-update) | async-done | bytes 1048592 | tf_op jit(solution)/shard_map/psum | solution.py:100
  150.3 2.5 multiply_reduce_fusion.5
  153.9 38.0 %while.61 = (s32[]{:T(128)}, f32[2,8,128,128]{3,2,1,0:T(8,128)}, s32[]{:T(128)}, s32[24]{0:T(128)S(1)}, bf16[24,2,128,128]{3,2,0,1:T(8,128)(2,1)S(1)}, /*index=5...) while((s32[]{:T(128)}, f32[2,8,128,128]{3,2,1,0:T(8,128)}, ...), condition=%wide.region_6.8_spmd, body=%wide.region_5.7_spmd.sunk | while | flops 135529568 | bytes 17834880 | solution.py:47
  160.6 2.3 fusion.368
  164.8 2.2 fusion.369
  169.1 2.1 fusion.370
  173.1 2.1 fusion.371
  177.4 2.2 fusion.372
  181.6 2.2 fusion.373
  185.8 2.3 fusion.374
  189.8 2.2 fusion.375
  192.0 92.6 %psum.85 = f32[128]{0:T(128)S(1)} all-reduce(f32[128]{0:T(128)S(1)} %get-tuple-element.527), channel_id=1, replica_groups=mesh['hyd'=4,'src'=8] {'src'}, use_global_device_ids=true, to_apply=%region_4.6 | all-reduce | flops 128 | bytes 1024 | tf_op jit(solution)/shard_map/psum | solution.py:101
  284.6 42.1 %all-reduce.9.cloned.1.call-done = f32[2,1024,128]{2,1,0:T(8,128)} async-done(((f32[2,1024,128]{2,1,0:T(8,128)}), f32[2,1024,128]{2,1,0:T(8,128)}) %all-reduce.9.cloned.1.call-update) | async-done | bytes 1048592 | tf_op jit(solution)/shard_map/psum | solution.py:113
  328.2 9.8 psum.87
  338.0 2.1 fusion.241
  341.2 41.8 %while.62 = (s32[]{:T(128)}, f32[2,8,128,128]{3,2,1,0:T(8,128)}, s32[]{:T(128)}, s32[24]{0:T(128)S(1)}, bf16[24,2,128,128]{2,3,0,1:T(8,128)(2,1)}, /*index=5*/s3...) while((s32[]{:T(128)}, f32[2,8,128,128]{3,2,1,0:T(8,128)}, ...), condition=%wide.region_11.13_spmd, body=%wide.region_10.12_spmd.sunk | while | flops 135529568 | bytes 17834880 | solution.py:81
  351.6 2.3 fusion.383
  355.9 2.2 fusion.384
  360.2 2.1 fusion.385
  364.2 2.1 fusion.386
  368.4 2.2 fusion.387
  372.7 2.2 fusion.388
  376.9 2.3 fusion.389
  380.8 2.2 fusion.390
  383.1 132.6 %all-reduce.11.cloned.1.call-done = f32[2,1024,128]{2,1,0:T(8,128)} async-done(((f32[2,1024,128]{2,1,0:T(8,128)}), f32[2,1024,128]{2,1,0:T(8,128)}) %all-reduce.11.cloned.1.call-update) | async-done | bytes 1048592 | tf_op jit(solution)/shard_map/psum | solution.py:100
  517.2 16.2 %psum.89 = f32[128]{0:T(128)S(1)} all-reduce(f32[128]{0:T(128)S(1)} %multiply_reduce_fusion.3), channel_id=1, replica_groups=mesh['hyd'=4,'src'=8] {'src'}, use_global_device_ids=true, to_apply=%region_14.16 | all-reduce | flops 128 | bytes 1024 | tf_op jit(solution)/shard_map/psum | solution.py:101
  533.4 2.1 fusion.242
  536.6 38.0 %while.63 = (s32[]{:T(128)}, f32[2,8,128,128]{3,2,1,0:T(8,128)}, s32[]{:T(128)}, s32[24]{0:T(128)S(1)}, bf16[24,2,128,128]{3,2,0,1:T(8,128)(2,1)S(1)}, /*index=5...) while((s32[]{:T(128)}, f32[2,8,128,128]{3,2,1,0:T(8,128)}, ...), condition=%wide.region_16.18_spmd, body=%wide.region_15.17_spmd.sunk | while | flops 135529568 | bytes 17834880 | solution.py:47
  543.6 2.2 fusion.398
  547.8 2.2 fusion.399
  552.0 2.2 fusion.400
  556.1 2.3 fusion.401
  564.2 2.2 fusion.403
  568.2 2.1 fusion.404
  572.3 2.3 fusion.405
  574.7 131.5 %all-reduce.13.cloned.1.call-done = f32[2,1024,128]{2,1,0:T(8,128)} async-done(((f32[2,1024,128]{2,1,0:T(8,128)}), f32[2,1024,128]{2,1,0:T(8,128)}) %all-reduce.13.cloned.1.call-update) | async-done | bytes 1048592 | tf_op jit(solution)/shard_map/psum | solution.py:113
  707.7 9.8 psum.91
  717.5 2.9 fusion.243
  721.4 41.1 %while.64 = (s32[]{:T(128)}, f32[2,8,128,128]{3,2,1,0:T(8,128)}, s32[]{:T(128)}, s32[24]{0:T(128)S(1)}, bf16[24,2,128,128]{2,3,0,1:T(8,128)(2,1)}, /*index=5*/s3...) while((s32[]{:T(128)}, f32[2,8,128,128]{3,2,1,0:T(8,128)}, ...), condition=%wide.region_21.23_spmd, body=%wide.region_20.22_spmd.sunk | while | flops 135529568 | bytes 17834880 | solution.py:81
  732.0 2.2 fusion.413
  736.0 2.3 fusion.414
  740.0 2.2 fusion.415
  743.9 2.1 fusion.416
  748.1 2.2 fusion.417
  752.1 2.2 fusion.418
  756.1 2.3 fusion.419
  760.3 2.2 fusion.420
  762.6 131.3 %all-reduce.15.cloned.1.call-done = f32[2,1024,128]{2,1,0:T(8,128)} async-done(((f32[2,1024,128]{2,1,0:T(8,128)}), f32[2,1024,128]{2,1,0:T(8,128)}) %all-reduce.15.cloned.1.call-update) | async-done | bytes 1048592 | tf_op jit(solution)/shard_map/psum | solution.py:100
  895.4 16.2 %psum.93 = f32[128]{0:T(128)S(1)} all-reduce(f32[128]{0:T(128)S(1)} %multiply_reduce_fusion.1), channel_id=1, replica_groups=mesh['hyd'=4,'src'=8] {'src'}, use_global_device_ids=true, to_apply=%region_24.26 | all-reduce | flops 128 | bytes 1024 | tf_op jit(solution)/shard_map/psum | solution.py:101
  911.6 2.5 fusion.240
  915.2 37.3 %while.65 = (s32[]{:T(128)}, f32[2,8,128,128]{3,2,1,0:T(8,128)}, s32[]{:T(128)}, s32[24]{0:T(128)S(1)}, bf16[24,2,128,128]{3,2,0,1:T(8,128)(2,1)S(1)}, /*index=5...) while((s32[]{:T(128)}, f32[2,8,128,128]{3,2,1,0:T(8,128)}, ...), condition=%wide.region_26.28_spmd, body=%wide.region_25.27_spmd.sunk | while | flops 135529568 | bytes 17834880 | solution.py:47
  921.9 2.2 fusion.428
  926.0 2.3 fusion.429
  930.0 2.2 fusion.430
  933.8 2.1 fusion.431
  938.0 2.2 fusion.432
  942.1 2.2 fusion.433
  946.1 2.3 fusion.434
  950.3 2.2 fusion.435
  952.5 130.2 %all-reduce.17.cloned.1.call-done = f32[2,1024,128]{2,1,0:T(8,128)} async-done(((f32[2,1024,128]{2,1,0:T(8,128)}), f32[2,1024,128]{2,1,0:T(8,128)}) %all-reduce.17.cloned.1.call-update) | async-done | bytes 1048592 | tf_op jit(solution)/shard_map/psum | solution.py:113
  1084.2 9.8 psum.95
  1094.0 3.6 multiply_subtract_fusion
  (125 shorter events, 63.3 us)
Async XLA Ops:
  7.2 143.2 %all-reduce.7.cloned.1.call-start = ((), (), s32[]{:S(2)}) async-start(), calls=%async_computation | async-start | bytes 2097152 | tf_op jit(solution)/shard_map/psum | solution.py:100
  7.9 2.7 copy-start.5
  10.6 0.7 copy-start.8
  10.6 0.7 copy-start.9
  39.3 1.0 copy-start
  40.3 286.4 %all-reduce.9.cloned.1.call-start = ((), (), s32[]{:S(2)}) async-start(), calls=%async_computation.1 | async-start | bytes 2097152 | tf_op jit(solution)/shard_map/psum | solution.py:113
  191.9 146.1 %copy-start.6 = (f32[2,1024,128]{2,1,0:T(8,128)S(1)}, f32[2,1024,128]{2,1,0:T(8,128)}, u32[]{:S(2)}) copy-start(f32[2,1024,128]{2,1,0:T(8,128)} %param.19) | copy-start | bytes 3145732
  192.0 323.8 %all-reduce.11.cloned.1.call-start = ((), (), s32[]{:S(2)}) async-start(), calls=%async_computation.2 | async-start | bytes 2097152 | tf_op jit(solution)/shard_map/psum | solution.py:100
  383.0 150.4 %copy-start.1 = (f32[2,1024,128]{2,1,0:T(8,128)S(1)}, f32[2,1024,128]{2,1,0:T(8,128)}, u32[]{:S(2)}) copy-start(f32[2,1024,128]{2,1,0:T(8,128)} %all-reduce.7.cloned.1.call-done) | copy-start | bytes 3145732
  383.0 323.1 %all-reduce.13.cloned.1.call-start = ((), (), s32[]{:S(2)}) async-start(), calls=%async_computation.3 | async-start | bytes 2097152 | tf_op jit(solution)/shard_map/psum | solution.py:113
  574.6 142.8 %copy-start.7 = (f32[2,1024,128]{2,1,0:T(8,128)S(1)}, f32[2,1024,128]{2,1,0:T(8,128)}, u32[]{:S(2)}) copy-start(f32[2,1024,128]{2,1,0:T(8,128)} %param.19) | copy-start | bytes 3145732
  574.6 319.2 %all-reduce.15.cloned.1.call-start = ((), (), s32[]{:S(2)}) async-start(), calls=%async_computation.4 | async-start | bytes 2097152 | tf_op jit(solution)/shard_map/psum | solution.py:100
  762.5 149.0 %copy-start.2 = (f32[2,1024,128]{2,1,0:T(8,128)S(1)}, f32[2,1024,128]{2,1,0:T(8,128)}, u32[]{:S(2)}) copy-start(f32[2,1024,128]{2,1,0:T(8,128)} %all-reduce.7.cloned.1.call-done) | copy-start | bytes 3145732
  762.6 320.1 %all-reduce.17.cloned.1.call-start = ((), (), s32[]{:S(2)}) async-start(), calls=%async_computation.5 | async-start | bytes 2097152 | tf_op jit(solution)/shard_map/psum | solution.py:113
  952.5 141.5 %copy-start.3 = (f32[2,1024,128]{2,1,0:T(8,128)S(1)}, f32[2,1024,128]{2,1,0:T(8,128)}, u32[]{:S(2)}) copy-start(f32[2,1024,128]{2,1,0:T(8,128)} %all-reduce.7.cloned.1.call-done) | copy-start | bytes 3145732
  952.5 141.5 %copy-start.4 = (f32[2,1024,128]{2,1,0:T(8,128)S(1)}, f32[2,1024,128]{2,1,0:T(8,128)}, u32[]{:S(2)}) copy-start(f32[2,1024,128]{2,1,0:T(8,128)} %all-reduce.11.cloned.1.call-done) | copy-start | bytes 3145732
Sparse Core Ops, SparseCore 0:
  40.4 109.8 all-reduce.6
  192.1 134.5 all-reduce.8
  383.1 132.5 all-reduce.10
  574.8 131.3 all-reduce.12
  762.7 131.1 all-reduce.14
  952.6 130.0 all-reduce.16
where the time goes:
time: 1110 us; the launch traced here: 1100 us
  waiting for transfers between devices  676 us (61%)
  blocking collectives  154 us (14%)
  other arithmetic  122 us (11%)
  loops' own time  91.6 us (8%)
  local copies, waits for them, and re-layouts  29 us (3%)
  matrix products  16.7 us (2%)
  between operations  14.9 us (1%)
    psum x3, waiting for transfers between devices, gradient_of(): gradient = lax.psum(partial_value, 'hyd')  372 us
    psum x3, waiting for transfers between devices, body(): image = lax.psum(forward_partial_value, 'src')  304 us
    psum x3, blocking collectives, gradient_of(): squares = lax.psum(jnp.sum(gradient * gradient, axis=(0, 1)), 'src')  125 us
    dynamic_update_slice x48, other arithmetic, place_tiles(): total = lax.dynamic_update_slice_in_dim(total, added, target[slot], 1)  93.1 us
    another operation x3, loops' own time, tile_forward(): lax.fori_loop(first_slot // group_slots, (end_slot + group_slots - 1) //...  45.9 us
    another operation x3, loops' own time, tile_adjoint(): lax.fori_loop(first_slot // group_slots, (end_slot + group_slots - 1) //...  45.7 us
    psum x3, blocking collectives, body(): image_sq = lax.psum(jnp.sum(image * image, axis=(0, 1)), 'hyd')  29.3 us
  transfers between devices with their start and end apart: 6, of which 6 were waited for; matrix products, arithmetic and copies ran while one was open for 0% of the time, Pallas kernels for 0%

commit v1 on v0

--- a/solution.py
+++ b/solution.py
@@ -1,3 +1,4 @@
+import functools
 import jax
 import jax.numpy as jnp
 from jax import lax
@@ -6,6 +7,20 @@
 SRC_DEV = 512
 ITERS = 3
 EPSILON = 1e-06
+
+
+def _play_heaps(xs, peer_axis):
+    width = lax.axis_size(peer_axis)
+    side_arr = lambda t_next: [(j, j ^ t_next) for j in range(width)]
+    parts_out = xs
+    for s in range(width.bit_length() - 1):
+        vec_out = side_arr(1 << s)
+        top = lax.ppermute(parts_out, peer_axis, vec_out)
+        parts_out = parts_out + top
+    return parts_out
+
+
+rest_the_series = functools.partial(_play_heaps, peer_axis="src")
 
 
 def place_tiles(total, products, target, usable):
@@ -110,7 +125,7 @@
         forward_partial_value = tile_forward(
             own_tiles, own_rows, own_cols, 0, own_count, direction_b, row_tiles
         )
-        image = lax.psum(forward_partial_value, "src")
+        image = rest_the_series(forward_partial_value)
         image_sq = lax.psum(jnp.sum(image * image, axis=(0, 1)), "hyd")
         image, image_sq = (image, image_sq)
         alpha_step = gamma_now / (image_sq + EPSILON)

time: 1110 us -> 1170 us (1.054)
  starting transfers between devices: 0.24 us -> 230 us
  waiting for transfers between devices: 676 us -> 560 us
  blocking collectives: 154 us -> 93.4 us
    psum x3 -> x0, waiting for transfers between devices: 304 us -> none  [body(): image = lax.psum(forward_partial_value, 'src')]
    ppermute x0 -> x9, starting transfers between devices: none -> 230 us  [_play_heaps(): top = lax.ppermute(parts_out, peer_axis, vec_out)]
    ppermute x0 -> x9, waiting for transfers between devices: none -> 182 us  [_play_heaps(): top = lax.ppermute(parts_out, peer_axis, vec_out)]
    psum x3, blocking collectives: 125 us -> 66.7 us  [gradient_of(): squares = lax.psum(jnp.sum(gradient * gradient, axis=(0, 1)), 'src')]
  transfers between devices with their start and end apart: 6 -> 12, of which waited for: 6 -> 12; matrix products, arithmetic and copies ran while one was open for 0% -> 0% of each run, Pallas kernels for 0% -> 0%
where the time goes in v1:
time: 1170 us; the launch traced here: 1160 us
  waiting for transfers between devices  560 us (48%)
  starting transfers between devices  230 us (20%)
  other arithmetic  130 us (11%)
  blocking collectives  93.4 us (8%)
  loops' own time  90.7 us (8%)
  local copies, waits for them, and re-layouts  29 us (2%)
  matrix products  16.7 us (1%)
  between operations  14.5 us (1%)
    psum x3, waiting for transfers between devices, gradient_of(): gradient = lax.psum(partial_value, 'hyd')  378 us
    ppermute x9, starting transfers between devices, _play_heaps(): top = lax.ppermute(parts_out, peer_axis, vec_out)  230 us
    ppermute x9, waiting for transfers between devices, _play_heaps(): top = lax.ppermute(parts_out, peer_axis, vec_out)  182 us
    dynamic_update_slice x48, other arithmetic, place_tiles(): total = lax.dynamic_update_slice_in_dim(total, added, target[slot], 1)  93.4 us
    psum x3, blocking collectives, gradient_of(): squares = lax.psum(jnp.sum(gradient * gradient, axis=(0, 1)), 'src')  66.7 us
    another operation x3, loops' own time, tile_adjoint(): lax.fori_loop(first_slot // group_slots, (end_slot + group_slots - 1) //...  46 us
    another operation x3, loops' own time, tile_forward(): lax.fori_loop(first_slot // group_slots, (end_slot + group_slots - 1) //...  44.7 us
    psum x3, blocking collectives, body(): image_sq = lax.psum(jnp.sum(image * image, axis=(0, 1)), 'hyd')  26.7 us
  transfers between devices with their start and end apart: 12, of which 12 were waited for; matrix products, arithmetic and copies ran while one was open for 0% of the time, Pallas kernels for 0%

profile of v1, /device:TPU:0, one launch (start us, length us, event | category | flops | bytes accessed | tf_op | source)
XLA Modules:
  0.0 1164.4 jit_solution(5365696861917652262)
XLA Ops:
  7.9 2.7 copy.18
  11.3 28.3 %while.60 = (s32[]{:T(128)}, f32[2,8,128,128]{3,2,1,0:T(8,128)S(1)}, s32[]{:T(128)}, s32[24]{0:T(128)S(1)}, bf16[24,2,128,128]{2,3,0,1:T(8,128)(2,1)}, /*index=5...) while((s32[]{:T(128)}, ...), condition=%wide.region_1.3_spmd, body=%wide.region_0.2_spmd.sunk | while | flops 135529568 | bytes 17830816 | solution.py:96
  42.3 109.0 %all-reduce.4.cloned.1.call-done = f32[2,1024,128]{2,1,0:T(8,128)} async-done(((f32[2,1024,128]{2,1,0:T(8,128)}), f32[2,1024,128]{2,1,0:T(8,128)}) %all-reduce.4.cloned.1.call-update) | async-done | bytes 1048592 | tf_op jit(solution)/shard_map/psum | solution.py:115
  151.2 2.5 multiply_reduce_fusion.5
  154.8 37.0 %while.61 = (s32[]{:T(128)}, f32[2,8,128,128]{3,2,1,0:T(8,128)}, s32[]{:T(128)}, s32[24]{0:T(128)S(1)}, bf16[24,2,128,128]{3,2,0,1:T(8,128)(2,1)S(1)}, /*index=5...) while((s32[]{:T(128)}, f32[2,8,128,128]{3,2,1,0:T(8,128)}, ...), condition=%wide.region_6.8_spmd, body=%wide.region_5.7_spmd.sunk | while | flops 135529568 | bytes 17834880 | solution.py:62
  165.5 2.3 fusion.369
  173.7 2.2 fusion.371
  189.6 2.2 fusion.375
  191.8 36.6 %collective-permute-start = (f32[2,1024,128]{2,1,0:T(8,128)}, f32[2,1024,128]{2,1,0:T(8,128)S(1)}, u32[]{:S(2)}, u32[]{:S(2)}) collective-permute-start(f32[2,1024,128]{2,1,0:T(8,128)} %bitcast.579), channel_id=1, source_target_pairs={{0,1},{1,0},{2,3},{3,2},{4,5},{5,4},{6,7},{7,6},{8,9},{9,8},{10,11... | collective-permute-start | bytes 3145736 | tf_op jit(solution)/shard_map/ppermute | solution.py:18
  228.4 2.5 collective-permute-done
  232.3 39.2 %collective-permute-start.1 = (f32[2,1024,128]{2,1,0:T(8,128)S(1)}, f32[2,1024,128]{2,1,0:T(8,128)S(1)}, u32[]{:S(2)}, u32[]{:S(2)}) collective-permute-start(f32[2,1024,128]{2,1,0:T(8,128)S(1)} %bitcast_add_fusion.2), channel_id=1, source_target_pairs={{0,2},{1,3},{2,0},{3,1},{4,6},{5,7},{6,4},{7,5},{8,10},{9,11},{10,... | collective-permute-start | bytes 3145736 | tf_op jit(solution)/shard_map/ppermute | solution.py:18
  271.5 23.5 %collective-permute-done.1 = f32[2,1024,128]{2,1,0:T(8,128)S(1)} collective-permute-done((f32[2,1024,128]{2,1,0:T(8,128)S(1)}, f32[2,1024,128]{2,1,0:T(8,128)S(1)}, u32[]{:S(2)}, u32[]{:S(2)}) %collective-permute-start.1) | collective-permute-done | bytes 1048608 | tf_op jit(solution)/shard_map/ppermute | solution.py:18
  298.0 34.4 %psum.64 = f32[128]{0:T(128)S(1)} all-reduce(f32[128]{0:T(128)S(1)} %get-tuple-element.533), channel_id=1, replica_groups=mesh['hyd'=4,'src'=8] {'src'}, use_global_device_ids=true, to_apply=%region_4.6 | all-reduce | flops 128 | bytes 1024 | tf_op jit(solution)/shard_map/psum | solution.py:116
  332.3 12.2 %collective-permute-done.2 = f32[2,1024,128]{2,1,0:T(8,128)} collective-permute-done((f32[2,1024,128]{2,1,0:T(8,128)}, f32[2,1024,128]{2,1,0:T(8,128)}, u32[]{:S(2)}, u32[]{:S(2)}) %collective-permute-start.2) | collective-permute-done | bytes 1048608 | tf_op jit(solution)/shard_map/ppermute | solution.py:18
  344.6 2.7 multiply_reduce_fusion.4
  347.3 8.9 psum.65
  359.4 41.5 %while.62 = (s32[]{:T(128)}, f32[2,8,128,128]{3,2,1,0:T(8,128)}, s32[]{:T(128)}, s32[24]{0:T(128)S(1)}, bf16[24,2,128,128]{2,3,0,1:T(8,128)(2,1)}, /*index=5*/s3...) while((s32[]{:T(128)}, f32[2,8,128,128]{3,2,1,0:T(8,128)}, ...), condition=%wide.region_10.12_spmd, body=%wide.region_9.11_spmd.sunk | while | flops 135529568 | bytes 17834880 | solution.py:96
  370.2 2.2 fusion.383
  374.1 2.2 fusion.384
  394.5 2.2 fusion.389
  398.6 2.3 fusion.390
  401.0 136.8 %all-reduce.6.cloned.1.call-done = f32[2,1024,128]{2,1,0:T(8,128)} async-done(((f32[2,1024,128]{2,1,0:T(8,128)}), f32[2,1024,128]{2,1,0:T(8,128)}) %all-reduce.6.cloned.1.call-update) | async-done | bytes 1048592 | tf_op jit(solution)/shard_map/psum | solution.py:115
  539.2 16.2 %psum.67 = f32[128]{0:T(128)S(1)} all-reduce(f32[128]{0:T(128)S(1)} %multiply_reduce_fusion.3), channel_id=1, replica_groups=mesh['hyd'=4,'src'=8] {'src'}, use_global_device_ids=true, to_apply=%region_13.15 | all-reduce | flops 128 | bytes 1024 | tf_op jit(solution)/shard_map/psum | solution.py:116
  558.6 37.7 %while.63 = (s32[]{:T(128)}, f32[2,8,128,128]{3,2,1,0:T(8,128)}, s32[]{:T(128)}, s32[24]{0:T(128)S(1)}, bf16[24,2,128,128]{3,2,0,1:T(8,128)(2,1)S(1)}, /*index=5...) while((s32[]{:T(128)}, f32[2,8,128,128]{3,2,1,0:T(8,128)}, ...), condition=%wide.region_15.17_spmd, body=%wide.region_14.16_spmd.sunk | while | flops 135529568 | bytes 17834880 | solution.py:62
  565.4 2.2 fusion.398
  569.6 2.2 fusion.399
  573.7 2.2 fusion.400
  577.8 2.3 fusion.401
  585.9 2.3 fusion.403
  589.9 2.3 fusion.404
  594.2 2.2 fusion.405
  596.4 35.0 %collective-permute-start.3 = (f32[2,1024,128]{2,1,0:T(8,128)}, f32[2,1024,128]{2,1,0:T(8,128)S(1)}, u32[]{:S(2)}, u32[]{:S(2)}) collective-permute-start(f32[2,1024,128]{2,1,0:T(8,128)} %bitcast.580), channel_id=1, source_target_pairs={{0,1},{1,0},{2,3},{3,2},{4,5},{5,4},{6,7},{7,6},{8,9},{9,8},{10,11... | collective-permute-start | bytes 3145736 | tf_op jit(solution)/shard_map/ppermute | solution.py:18
  631.4 2.5 collective-permute-done.3
  635.2 38.9 %collective-permute-start.4 = (f32[2,1024,128]{2,1,0:T(8,128)S(1)}, f32[2,1024,128]{2,1,0:T(8,128)S(1)}, u32[]{:S(2)}, u32[]{:S(2)}) collective-permute-start(f32[2,1024,128]{2,1,0:T(8,128)S(1)} %bitcast_add_fusion.1), channel_id=1, source_target_pairs={{0,2},{1,3},{2,0},{3,1},{4,6},{5,7},{6,4},{7,5},{8,10},{9,11},{10,... | collective-permute-start | bytes 3145736 | tf_op jit(solution)/shard_map/ppermute | solution.py:18
  674.1 23.5 %collective-permute-done.4 = f32[2,1024,128]{2,1,0:T(8,128)S(1)} collective-permute-done((f32[2,1024,128]{2,1,0:T(8,128)S(1)}, f32[2,1024,128]{2,1,0:T(8,128)S(1)}, u32[]{:S(2)}, u32[]{:S(2)}) %collective-permute-start.4) | collective-permute-done | bytes 1048608 | tf_op jit(solution)/shard_map/ppermute | solution.py:18
  698.6 2.3 collective-permute-start.5
  700.9 46.0 %collective-permute-done.5 = f32[2,1024,128]{2,1,0:T(8,128)} collective-permute-done((f32[2,1024,128]{2,1,0:T(8,128)}, f32[2,1024,128]{2,1,0:T(8,128)}, u32[]{:S(2)}, u32[]{:S(2)}) %collective-permute-start.5) | collective-permute-done | bytes 1048608 | tf_op jit(solution)/shard_map/ppermute | solution.py:18
  746.9 2.7 multiply_reduce_fusion.2
  749.7 8.9 psum.68
  758.6 2.9 fusion.243
  762.5 41.5 %while.64 = (s32[]{:T(128)}, f32[2,8,128,128]{3,2,1,0:T(8,128)}, s32[]{:T(128)}, s32[24]{0:T(128)S(1)}, bf16[24,2,128,128]{2,3,0,1:T(8,128)(2,1)}, /*index=5*/s3...) while((s32[]{:T(128)}, f32[2,8,128,128]{3,2,1,0:T(8,128)}, ...), condition=%wide.region_19.21_spmd, body=%wide.region_18.20_spmd.sunk | while | flops 135529568 | bytes 17834880 | solution.py:96
  773.1 2.2 fusion.413
  777.3 2.2 fusion.414
  785.5 2.3 fusion.416
  793.6 2.3 fusion.418
  797.6 2.3 fusion.419
  801.9 2.2 fusion.420
  804.1 132.6 %all-reduce.8.cloned.1.call-done = f32[2,1024,128]{2,1,0:T(8,128)} async-done(((f32[2,1024,128]{2,1,0:T(8,128)}), f32[2,1024,128]{2,1,0:T(8,128)}) %all-reduce.8.cloned.1.call-update) | async-done | bytes 1048592 | tf_op jit(solution)/shard_map/psum | solution.py:115
  938.2 16.2 %psum.70 = f32[128]{0:T(128)S(1)} all-reduce(f32[128]{0:T(128)S(1)} %multiply_reduce_fusion.1), channel_id=1, replica_groups=mesh['hyd'=4,'src'=8] {'src'}, use_global_device_ids=true, to_apply=%region_22.24 | all-reduce | flops 128 | bytes 1024 | tf_op jit(solution)/shard_map/psum | solution.py:116
  954.4 2.5 fusion.240
  958.0 37.4 %while.65 = (s32[]{:T(128)}, f32[2,8,128,128]{3,2,1,0:T(8,128)}, s32[]{:T(128)}, s32[24]{0:T(128)S(1)}, bf16[24,2,128,128]{3,2,0,1:T(8,128)(2,1)S(1)}, /*index=5...) while((s32[]{:T(128)}, f32[2,8,128,128]{3,2,1,0:T(8,128)}, ...), condition=%wide.region_24.26_spmd, body=%wide.region_23.25_spmd.sunk | while | flops 135529568 | bytes 17834880 | solution.py:62
  964.7 2.2 fusion.428
  968.6 2.3 fusion.429
  976.7 2.2 fusion.431
  980.8 2.2 fusion.432
  989.1 2.3 fusion.434
  995.5 34.7 %collective-permute-start.6 = (f32[2,1024,128]{2,1,0:T(8,128)}, f32[2,1024,128]{2,1,0:T(8,128)S(1)}, u32[]{:S(2)}, u32[]{:S(2)}) collective-permute-start(f32[2,1024,128]{2,1,0:T(8,128)} %bitcast.578), channel_id=1, source_target_pairs={{0,1},{1,0},{2,3},{3,2},{4,5},{5,4},{6,7},{7,6},{8,9},{9,8},{10,11... | collective-permute-start | bytes 3145736 | tf_op jit(solution)/shard_map/ppermute | solution.py:18
  1030.2 2.5 collective-permute-done.6
  1034.0 38.6 %collective-permute-start.7 = (f32[2,1024,128]{2,1,0:T(8,128)S(1)}, f32[2,1024,128]{2,1,0:T(8,128)S(1)}, u32[]{:S(2)}, u32[]{:S(2)}) collective-permute-start(f32[2,1024,128]{2,1,0:T(8,128)S(1)} %bitcast_add_fusion), channel_id=1, source_target_pairs={{0,2},{1,3},{2,0},{3,1},{4,6},{5,7},{6,4},{7,5},{8,10},{9,11},{10,... | collective-permute-start | bytes 3145736 | tf_op jit(solution)/shard_map/ppermute | solution.py:18
  1072.6 23.5 %collective-permute-done.7 = f32[2,1024,128]{2,1,0:T(8,128)S(1)} collective-permute-done((f32[2,1024,128]{2,1,0:T(8,128)S(1)}, f32[2,1024,128]{2,1,0:T(8,128)S(1)}, u32[]{:S(2)}, u32[]{:S(2)}) %collective-permute-start.7) | collective-permute-done | bytes 1048608 | tf_op jit(solution)/shard_map/ppermute | solution.py:18
  1096.2 2.4 collective-permute-start.8
  1098.6 45.7 %collective-permute-done.8 = f32[2,1024,128]{2,1,0:T(8,128)S(1)} collective-permute-done((f32[2,1024,128]{2,1,0:T(8,128)S(1)}, f32[2,1024,128]{2,1,0:T(8,128)S(1)}, u32[]{:S(2)}, u32[]{:S(2)}) %collective-permute-start.8) | collective-permute-done | bytes 1048608 | tf_op jit(solution)/shard_map/ppermute | solution.py:18
  1145.4 8.9 psum.71
  1154.3 3.6 multiply_subtract_fusion
  (140 shorter events, 102.5 us)
Async XLA Ops:
  7.2 144.0 %all-reduce.4.cloned.1.call-start = ((), (), s32[]{:S(2)}) async-start(), calls=%async_computation | async-start | bytes 2097152 | tf_op jit(solution)/shard_map/psum | solution.py:115
  7.9 2.7 copy-start.5
  10.6 0.7 copy-start.8
  10.6 0.7 copy-start.9
  39.6 1.0 copy-start
  40.6 497.1 %all-reduce.6.cloned.1.call-start = ((), (), s32[]{:S(2)}) async-start(), calls=%async_computation.1 | async-start | bytes 2097152 | tf_op jit(solution)/shard_map/psum | solution.py:115
  191.8 39.1 %collective-permute-start = (f32[2,1024,128]{2,1,0:T(8,128)}, f32[2,1024,128]{2,1,0:T(8,128)S(1)}, u32[]{:S(2)}, u32[]{:S(2)}) collective-permute-start(f32[2,1024,128]{2,1,0:T(8,128)} %bitcast.579), channel_id=1, source_target_pairs={{0,1},{1,0},{2,3},{3,2},{4,5},{5,4},{6,7},{7,6},{8,9},{9,8},{10,11... | collective-permute-start | bytes 3145736 | tf_op jit(solution)/shard_map/ppermute | solution.py:18
  232.3 62.7 %collective-permute-start.1 = (f32[2,1024,128]{2,1,0:T(8,128)S(1)}, f32[2,1024,128]{2,1,0:T(8,128)S(1)}, u32[]{:S(2)}, u32[]{:S(2)}) collective-permute-start(f32[2,1024,128]{2,1,0:T(8,128)S(1)} %bitcast_add_fusion.2), channel_id=1, source_target_pairs={{0,2},{1,3},{2,0},{3,1},{4,6},{5,7},{6,4},{7,5},{8,10},{9,11},{10,... | collective-permute-start | bytes 3145736 | tf_op jit(solution)/shard_map/ppermute | solution.py:18
  296.0 48.5 %collective-permute-start.2 = (f32[2,1024,128]{2,1,0:T(8,128)}, f32[2,1024,128]{2,1,0:T(8,128)}, u32[]{:S(2)}, u32[]{:S(2)}) collective-permute-start(f32[2,1024,128]{2,1,0:T(8,128)} %add.524), channel_id=1, source_target_pairs={{0,4},{1,5},{2,6},{3,7},{4,0},{5,1},{6,2},{7,3},{8,12},{9,13},{10,... | collective-permute-start | bytes 3145736 | tf_op jit(solution)/shard_map/ppermute | solution.py:18
  332.3 23.8 %copy-start.6 = (f32[2,1024,128]{2,1,0:T(8,128)S(1)}, f32[2,1024,128]{2,1,0:T(8,128)}, u32[]{:S(2)}) copy-start(f32[2,1024,128]{2,1,0:T(8,128)} %param.19) | copy-start | bytes 3145732
  400.9 154.6 %copy-start.1 = (f32[2,1024,128]{2,1,0:T(8,128)S(1)}, f32[2,1024,128]{2,1,0:T(8,128)}, u32[]{:S(2)}) copy-start(f32[2,1024,128]{2,1,0:T(8,128)} %all-reduce.4.cloned.1.call-done) | copy-start | bytes 3145732
  400.9 535.8 %all-reduce.8.cloned.1.call-start = ((), (), s32[]{:S(2)}) async-start(), calls=%async_computation.2 | async-start | bytes 2097152 | tf_op jit(solution)/shard_map/psum | solution.py:115
  596.4 37.5 %collective-permute-start.3 = (f32[2,1024,128]{2,1,0:T(8,128)}, f32[2,1024,128]{2,1,0:T(8,128)S(1)}, u32[]{:S(2)}, u32[]{:S(2)}) collective-permute-start(f32[2,1024,128]{2,1,0:T(8,128)} %bitcast.580), channel_id=1, source_target_pairs={{0,1},{1,0},{2,3},{3,2},{4,5},{5,4},{6,7},{7,6},{8,9},{9,8},{10,11... | collective-permute-start | bytes 3145736 | tf_op jit(solution)/shard_map/ppermute | solution.py:18
  635.2 62.3 %collective-permute-start.4 = (f32[2,1024,128]{2,1,0:T(8,128)S(1)}, f32[2,1024,128]{2,1,0:T(8,128)S(1)}, u32[]{:S(2)}, u32[]{:S(2)}) collective-permute-start(f32[2,1024,128]{2,1,0:T(8,128)S(1)} %bitcast_add_fusion.1), channel_id=1, source_target_pairs={{0,2},{1,3},{2,0},{3,1},{4,6},{5,7},{6,4},{7,5},{8,10},{9,11},{10,... | collective-permute-start | bytes 3145736 | tf_op jit(solution)/shard_map/ppermute | solution.py:18
  698.6 48.3 %collective-permute-start.5 = (f32[2,1024,128]{2,1,0:T(8,128)}, f32[2,1024,128]{2,1,0:T(8,128)}, u32[]{:S(2)}, u32[]{:S(2)}) collective-permute-start(f32[2,1024,128]{2,1,0:T(8,128)} %add.530), channel_id=1, source_target_pairs={{0,4},{1,5},{2,6},{3,7},{4,0},{5,1},{6,2},{7,3},{8,12},{9,13},{10,... | collective-permute-start | bytes 3145736 | tf_op jit(solution)/shard_map/ppermute | solution.py:18
  700.9 57.6 %copy-start.7 = (f32[2,1024,128]{2,1,0:T(8,128)S(1)}, f32[2,1024,128]{2,1,0:T(8,128)}, u32[]{:S(2)}) copy-start(f32[2,1024,128]{2,1,0:T(8,128)} %param.19) | copy-start | bytes 3145732
  804.1 150.3 %copy-start.2 = (f32[2,1024,128]{2,1,0:T(8,128)S(1)}, f32[2,1024,128]{2,1,0:T(8,128)}, u32[]{:S(2)}) copy-start(f32[2,1024,128]{2,1,0:T(8,128)} %all-reduce.4.cloned.1.call-done) | copy-start | bytes 3145732
  995.5 37.2 %collective-permute-start.6 = (f32[2,1024,128]{2,1,0:T(8,128)}, f32[2,1024,128]{2,1,0:T(8,128)S(1)}, u32[]{:S(2)}, u32[]{:S(2)}) collective-permute-start(f32[2,1024,128]{2,1,0:T(8,128)} %bitcast.578), channel_id=1, source_target_pairs={{0,1},{1,0},{2,3},{3,2},{4,5},{5,4},{6,7},{7,6},{8,9},{9,8},{10,11... | collective-permute-start | bytes 3145736 | tf_op jit(solution)/shard_map/ppermute | solution.py:18
  1034.0 62.0 %collective-permute-start.7 = (f32[2,1024,128]{2,1,0:T(8,128)S(1)}, f32[2,1024,128]{2,1,0:T(8,128)S(1)}, u32[]{:S(2)}, u32[]{:S(2)}) collective-permute-start(f32[2,1024,128]{2,1,0:T(8,128)S(1)} %bitcast_add_fusion), channel_id=1, source_target_pairs={{0,2},{1,3},{2,0},{3,1},{4,6},{5,7},{6,4},{7,5},{8,10},{9,11},{10,... | collective-permute-start | bytes 3145736 | tf_op jit(solution)/shard_map/ppermute | solution.py:18
  1096.2 58.2 %copy-start.3 = (f32[2,1024,128]{2,1,0:T(8,128)S(1)}, f32[2,1024,128]{2,1,0:T(8,128)}, u32[]{:S(2)}) copy-start(f32[2,1024,128]{2,1,0:T(8,128)} %all-reduce.4.cloned.1.call-done) | copy-start | bytes 3145732
  1096.2 58.2 %copy-start.4 = (f32[2,1024,128]{2,1,0:T(8,128)S(1)}, f32[2,1024,128]{2,1,0:T(8,128)}, u32[]{:S(2)}) copy-start(f32[2,1024,128]{2,1,0:T(8,128)} %all-reduce.6.cloned.1.call-done) | copy-start | bytes 3145732
  1096.2 48.1 %collective-permute-start.8 = (f32[2,1024,128]{2,1,0:T(8,128)S(1)}, f32[2,1024,128]{2,1,0:T(8,128)S(1)}, u32[]{:S(2)}, u32[]{:S(2)}) collective-permute-start(f32[2,1024,128]{2,1,0:T(8,128)S(1)} %add.537), channel_id=1, source_target_pairs={{0,4},{1,5},{2,6},{3,7},{4,0},{5,1},{6,2},{7,3},{8,12},{9,13},{10,... | collective-permute-start | bytes 3145736 | tf_op jit(solution)/shard_map/ppermute | solution.py:18
Sparse Core Ops, SparseCore 0:
  40.7 110.4 all-reduce.3
  401.0 136.6 all-reduce.5
  804.2 132.4 all-reduce.7
